TPU v7x, 32 devices: a whole 2x2x4 slice. The times are simulated.
32 devices in a mesh: ctx: 8 (over y, x, core), tp: 4 (over z).
Axes of the slice: x: 2, y: 2, z: 4, core: 2. Of those that a mesh axis runs over, the one named last changes fastest.
Arguments:
- patches: bfloat16 [4096, 1280], P('ctx'), may hold values from -21 to 21
- window_ids: int32 [4096], P('ctx'), may hold values from -1 to 1023, as said below
- positions: int32 [1024], P('ctx'), may hold values from 0 to 8192, as said below
- text_embed: bfloat16 [8192, 8192], P('ctx', 'tp'), may hold values from -6 to 6
- cotangent: bfloat16 [8192, 8192], P('ctx', 'tp'), may hold values from -0.119628906 to 0.119628906
- qkv_weight: bfloat16 [3, 1280, 1280], P(None, None, 'tp'), may hold values from -0.15625 to 0.15625
- out_weight: bfloat16 [1280, 1280], P('tp'), may hold values from -0.15625 to 0.15625
- merger_weight: bfloat16 [5120, 8192], P('ctx', 'tp'), may hold values from -0.078125 to 0.078125
- norm_gain: bfloat16 [8192], P('tp'), may hold values from 0.099609375 to 1.8984375
Outputs:
- normed: bfloat16 [8192, 8192], P('ctx', 'tp')
- merger_grad: float32 [5120, 8192], P('ctx', 'tp')
Inputs may be any that keep to these rules, and one draw needn't show every extreme that they name: `window_ids`: windows are runs of consecutive patch slots of one index of ctx, each of 4 to 64 slots and a multiple of 4; every window id belongs to one index of ctx; the padding slots of an index of ctx come after its live slots and carry -1. Merged slot j of an index of ctx covers its patch slots 4j to 4j+3 and is live exactly when those are; live slots carry distinct positions, dead ones carry 8192. The live slots of one index of ctx name at most 16 positions among the 1024 positions of any one index of ctx.
All inputs are finite; a program needn't handle non-finite values.
Results may differ from a plain program's by a relative error of at most 0.014.
Values may be sent and summed in bfloat16 or wider, within the bound.
No kernel may reach another device: no remote copies, remote signals or barrier semaphores. Data moves between devices by JAX's collectives and lax.ppermute only.
A program may use at most 128 MiB of HBM per device.

v0:
```python
import jax
import jax.numpy as jnp
from jax import lax
from jax.sharding import PartitionSpec as P

D = 8192
HEAD_DIM = 80


def window_attention(patches, window_ids, qkv_weight):
    slot_rows = patches.shape[0]
    projected = [
        jnp.dot(patches, qkv_weight[i], preferred_element_type=jnp.float32).astype(jnp.bfloat16)
        for i in range(3)
    ]
    local_heads = qkv_weight.shape[2] // HEAD_DIM
    queries = projected[0].reshape(slot_rows, local_heads, HEAD_DIM)
    keys_all = projected[1].reshape(slot_rows, local_heads, HEAD_DIM)
    values = projected[2].reshape(slot_rows, local_heads, HEAD_DIM)
    width = min(512, slot_rows)
    factor = 1.0 / HEAD_DIM**0.5

    def one_block(block_index):
        scores = (
            jnp.einsum("qhd,khd->hqk", queries, keys_all, preferred_element_type=jnp.float32)
            * factor
        )
        allowed = (window_ids[:, None] == window_ids[None, :]) & (window_ids[None, :] >= 0)
        scores = jnp.where(allowed[None], scores, jnp.float32(-1e30))
        highest = jnp.max(scores, axis=2, keepdims=True)
        weights = jnp.exp(scores - highest)
        probs = (weights / jnp.sum(weights, axis=2, keepdims=True)).astype(jnp.bfloat16)
        attended = jnp.einsum("hqk,khd->qhd", probs, values, preferred_element_type=jnp.float32)
        return attended.astype(jnp.bfloat16).reshape(width, local_heads * HEAD_DIM)

    blocks = lax.map(one_block, jnp.arange(slot_rows // width, dtype=jnp.int32))
    return blocks.reshape(slot_rows, local_heads * HEAD_DIM)


def contract_rows(left, right):
    return lax.dot_general(
        left, right, (((0,), (0,)), ((), ())), preferred_element_type=jnp.float32
    )


def shards(
    patches,
    window_ids,
    positions,
    text_embed,
    cotangent,
    qkv_weight,
    out_weight,
    merger_weight,
    norm_gain,
):
    ctx_size = lax.axis_size("ctx")
    slots = positions.shape[0]
    tok_rows = text_embed.shape[0]
    bucket_size = slots // ctx_size
    attended = window_attention(patches, window_ids, qkv_weight)
    partial_out = jnp.dot(attended, out_weight, preferred_element_type=jnp.float32)
    summed = lax.psum(partial_out.astype(jnp.bfloat16), "tp").astype(jnp.float32)
    hidden = (patches.astype(jnp.float32) + summed).astype(jnp.bfloat16)
    merged_in = hidden.reshape(slots, 4 * hidden.shape[1])
    columns = lax.all_to_all(merged_in, "ctx", split_axis=1, concat_axis=0, tiled=True)
    chosen = merged_in
    merged = jnp.dot(
        chosen,
        lax.all_gather(merger_weight, "ctx", axis=0, tiled=True),
        preferred_element_type=jnp.float32,
    ).astype(jnp.bfloat16)
    target = positions // tok_rows
    hits = (target[:, None] == jnp.arange(ctx_size, dtype=jnp.int32)[None, :]).astype(jnp.int32)
    ranks = jnp.sum(jnp.cumsum(hits, axis=0) * hits, axis=1) - 1
    bucket = jnp.where(target < ctx_size, target * bucket_size + ranks, -1)
    select = jnp.arange(slots, dtype=jnp.int32)[:, None] == bucket[None, :]
    select_mat = select.astype(jnp.bfloat16)
    outgoing = jnp.dot(select_mat, merged, preferred_element_type=jnp.float32).astype(jnp.bfloat16)
    local_row = positions % tok_rows
    occupied = jnp.any(select, axis=1)
    out_rows = jnp.where(occupied, jnp.sum(jnp.where(select, local_row[None, :], 0), axis=1), -1)
    incoming, in_rows = (
        lax.all_to_all(outgoing, "ctx", split_axis=0, concat_axis=0, tiled=True),
        lax.all_to_all(out_rows, "ctx", split_axis=0, concat_axis=0, tiled=True),
    )
    placed = jnp.arange(tok_rows, dtype=jnp.int32)[:, None] == in_rows[None, :]
    placed_mat = placed.astype(jnp.bfloat16)
    vision = jnp.dot(placed_mat, incoming, preferred_element_type=jnp.float32)
    is_vision = jnp.any(placed, axis=1)
    embedded = jnp.where(is_vision[:, None], vision, text_embed.astype(jnp.float32))
    gain_vec = norm_gain.astype(jnp.float32)[None, :]
    gained = gain_vec * cotangent.astype(jnp.float32)
    squares, inner = lax.psum(
        (jnp.sum(embedded * embedded, axis=1), jnp.sum(embedded * gained, axis=1)), "tp"
    )
    scale = lax.rsqrt(squares / D + 1e-06)[:, None]
    normed = (embedded * scale * gain_vec).astype(jnp.bfloat16)
    d_embed = (scale * gained - embedded * scale**3 * inner[:, None] / D).astype(jnp.bfloat16)
    back_rows = contract_rows(placed_mat, d_embed).astype(jnp.bfloat16)
    returned = lax.all_to_all(back_rows, "ctx", split_axis=0, concat_axis=0, tiled=True)
    d_merged = contract_rows(select_mat, returned).astype(jnp.bfloat16)
    chosen = columns
    merger_grad = contract_rows(chosen, lax.all_gather(d_merged, "ctx", axis=0, tiled=True))
    return (normed, merger_grad)


def solution(mesh):
    in_specs = (
        P("ctx", None),
        P("ctx"),
        P("ctx"),
        P("ctx", "tp"),
        P("ctx", "tp"),
        P(None, None, "tp"),
        P("tp", None),
        P("ctx", "tp"),
        P("tp"),
    )
    out_specs = (P("ctx", "tp"), P("ctx", "tp"))
    return jax.shard_map(shards, mesh=mesh, in_specs=in_specs, out_specs=out_specs, check_vma=False)
```

profile of v0, /device:TPU:0, one launch (start us, length us, event | category | flops | bytes accessed | tf_op | source)
XLA Modules:
  0.0 256.8 jit_solution(3629582103694238064)
XLA Ops:
  8.0 0.0 copy-start
  8.0 0.0 copy-start.2
  8.0 0.0 all-reduce.3.cloned.1.call-start
  8.1 2.3 convolution_convert_fusion.5
  10.4 2.2 convolution_convert_fusion.4
  12.6 1.8 convolution_convert_fusion.6
  14.4 0.2 compare_and_fusion
  14.6 3.8 %fusion.27 = (f32[4,512]{1,0:T(4,128)S(1)}, f32[4,512,512]{1,2,0:T(8,128)}) fusion(pred[512,512]{0,1:T(8,128)(4,1)S(1)} %compare_and_fusion, bf16[512,4,80]{0,2,1:T(8,128)(2,1)S(1)} %bitcast.45, bf16[512,4,80]{0,2,1:T(8,128)(2,1)S(1)} %bitcast.46), kind=kOutput, calls=%fused_computation.59 | convolution fusion | flops 171966976 | bytes 5120000 | tf_op jit(solution)/shard_map/while/body/eval_jaxpr/sub | solution.py:31
  18.4 2.7 %fusion.8 = bf16[4,80,512]{2,1,0:T(8,128)(2,1)S(1)} fusion(bf16[512,4,80]{0,2,1:T(8,128)(2,1)S(1)} %bitcast.44, f32[4,512,512]{1,2,0:T(8,128)} %get-tuple-element.29, f32[4,512]{1,0:T(4,128)S(1)} %get-tuple-element.28), kind=kOutput, calls=%fused_computation.25 | convolution fusion | flops 170033152 | bytes 4857856 | tf_op jit(solution)/shard_map/while/body/eval_jaxpr/hqk,khd->qhd/dot_general | solution.py:33
  21.1 0.0 copy-start.5
  21.1 1.9 convolution_convert_fusion
  23.0 0.0 all-reduce.3.cloned.1.call-update
  23.0 0.0 all-gather.3.cloned.1.call-start
  23.1 0.5 all-gather.3.cloned.1.call-update
  23.7 0.1 fusion.20
  23.7 0.2 reduce_window_sum.11
  23.9 0.2 select_reduce_fusion.1
  24.1 0.1 fusion.21
  24.2 0.1 select_reduce_fusion
  24.4 0.7 select_n.47
  25.0 5.2 %all-to-all-start = ((s32[8,16,1]{1,2,0:T(1,128)}), s32[8,16,1]{1,2,0:T(1,128)S(1)}, u32[]{:S(2)}, u32[]{:S(2)}) async-start(s32[8,16,1]{1,2,0:T(1,128)} %bitcast), calls=%async_computation | async-start | bytes 8192 | tf_op jit(solution)/shard_map/all_to_all | solution.py:85
  30.2 55.8 %all-reduce.3.cloned.1.call-done = bf16[512,1280]{1,0:T(8,128)(2,1)} async-done(((bf16[512,1280]{1,0:T(8,128)(2,1)}), bf16[512,1280]{1,0:T(8,128)(2,1)}) %all-reduce.3.cloned.1.call-update) | async-done | bytes 1310736 | tf_op jit(solution)/shard_map/psum | solution.py:63
  86.0 1.6 add_convert_fusion
  87.6 0.8 reshape.114
  88.5 0.0 copy-start.4
  88.5 47.0 %all-gather.3.cloned.1.call-done = bf16[5120,2048]{1,0:T(8,128)(2,1)} async-done(((bf16[640,2048]{1,0:T(8,128)(2,1)}), bf16[5120,2048]{1,0:T(8,128)(2,1)}) %all-gather.3.cloned.1.call-update) | async-done | bytes 20971536 | tf_op jit(solution)/shard_map/all_gather | solution.py:70
  135.5 10.9 %convolution_convert_fusion.2 = bf16[128,2048]{1,0:T(8,128)(2,1)} fusion(bf16[128,5120]{1,0:T(8,128)(2,1)S(1)} %reshape.114, bf16[5120,2048]{1,0:T(8,128)(2,1)} %all-gather.3.cloned.1.call-done, s32[128]{0:T(128)S(1)} %compare_select_fusion), kind=kOutput, calls=%fused_computation.16 | convolution fusion | flops 2752004096 | bytes 22807040 | tf_op jit(solution)/shard_map/dot_general | solution.py:79
  146.4 0.0 all-to-all-done
  146.4 3.5 %all-to-all-start.1 = ((bf16[8,16,2048]{2,1,0:T(8,128)(2,1)}), bf16[8,16,2048]{2,1,0:T(8,128)(2,1)S(1)}, u32[]{:S(2)}, u32[]{:S(2)}) async-start(bf16[8,16,2048]{2,1,0:T(8,128)(2,1)} %bitcast.9), calls=%async_computation.1 | async-start | bytes 1048576 | tf_op jit(solution)/shard_map/all_to_all | solution.py:84
  149.9 0.0 all-gather.5.cloned.1.call-start
  150.0 0.5 broadcast.108
  150.5 0.7 reduce.3
  151.1 0.1 eq.74
  151.2 0.2 fusion.15
  151.5 8.1 %all-to-all-done.1 = bf16[8,16,2048]{2,1,0:T(8,128)(2,1)S(1)} async-done(((bf16[8,16,2048]{2,1,0:T(8,128)(2,1)}), bf16[8,16,2048]{2,1,0:T(8,128)(2,1)S(1)}, u32[]{:S(2)}, u32[]{:S(2)}) %all-to-all-start.1) | async-done | bytes 524320 | tf_op jit(solution)/shard_map/all_to_all | solution.py:84
  159.5 7.1 %multiply_reduce_fusion = (f32[1024]{0:T(1024)S(1)}, f32[1024]{0:T(1024)S(1)}, f32[1024,2048]{1,0:T(8,128)}) fusion(bf16[1024,2048]{1,0:T(8,128)(2,1)} %param.13, f32[2048]{0:T(1024)S(1)} %convert_element_type.78, bf16[1024,2048]{1,0:T(8,128)(2,1)} %param.12, bf16[128,2048]{1,0:T(8,128)(2,1)S(1)} %bitcast.42, s32[128]{0:T(128)S(1)} %eq.74, ...), kind=kOutput, calls=%fused_computation.2 | convolution fusion | flops 553777152 | bytes 17319424 | tf_op jit(solution)/shard_map/dot_general | solution.py:89
  166.6 12.0 %all-reduce = (f32[1024]{0:T(1024)S(1)}, f32[1024]{0:T(1024)S(1)}) all-reduce(f32[1024]{0:T(1024)S(1)} %get-tuple-element.15, f32[1024]{0:T(1024)S(1)} %get-tuple-element.14), channel_id=1, replica_groups=mesh['ctx'=8,'tp'=4] {'tp'}, use_global_device_ids=true, to_apply=%region_9.10 | all-reduce | flops 2048 | bytes 16384 | tf_op jit(solution)/shard_map/psum | solution.py:94
  178.6 6.2 %fusion.3 = bf16[128,2048]{1,0:T(8,128)(2,1)S(1)} fusion(f32[1024,2048]{1,0:T(8,128)} %get-tuple-element.30, bf16[1024,2048]{1,0:T(8,128)(2,1)} %param.13, f32[1024]{0:T(1024)S(1)} %get-tuple-element.17, f32[1024]{0:T(1024)S(1)} %get-tuple-element.24, f32[2048]{0:T(1024)S(1)} %convert_element_type.78, f32[1024]{0:T(1024)S(1)} %get-tuple-element.25, ...), kind=kOutput, calls=%fused_computation.14 | convolution fusion | flops 554041344 | bytes 13128192 | tf_op jit(solution)/shard_map/dot_general | solution.py:41
  184.8 12.1 %all_to_all.49 = bf16[8,16,2048]{2,1,0:T(8,128)(2,1)S(1)} all-to-all(bf16[8,16,2048]{2,1,0:T(8,128)(2,1)S(1)} %bitcast.43), channel_id=1, replica_groups=mesh['ctx'=8,'tp'=4] {'ctx'}, dimensions={0} | all-to-all | bytes 1048576 | tf_op jit(solution)/shard_map/all_to_all | solution.py:101
  196.9 1.2 convolution_convert_fusion.1
  198.1 0.0 all-gather.5.cloned.1.call-update
  198.1 0.5 all_to_all.38
  198.6 1.2 copy.19
  199.8 3.6 %all-to-all-start.2 = ((bf16[128,8,640]{2,0,1:T(8,128)(2,1)}), bf16[128,8,640]{2,0,1:T(8,128)(2,1)S(1)}, u32[]{:S(2)}, u32[]{:S(2)}) async-start(bf16[128,8,640]{2,0,1:T(8,128)(2,1)} %copy.19), calls=%async_computation.2 | async-start | bytes 2621440 | tf_op jit(solution)/shard_map/all_to_all | solution.py:66
  203.4 6.2 %multiply_convert_fusion = bf16[1024,2048]{1,0:T(8,128)(2,1)} fusion(f32[1024,2048]{1,0:T(8,128)} %get-tuple-element.30, f32[2048]{0:T(1024)S(1)} %convert_element_type.78, f32[1024]{0:T(1024)S(1)} %get-tuple-element.25), kind=kLoop, calls=%fused_computation.4 | loop fusion | flops 6291456 | bytes 12595200 | tf_op jit(solution)/shard_map/convert_element_type | solution.py:98
  209.6 15.6 %all-to-all-done.2 = bf16[128,8,640]{2,0,1:T(8,128)(2,1)S(1)} async-done(((bf16[128,8,640]{2,0,1:T(8,128)(2,1)}), bf16[128,8,640]{2,0,1:T(8,128)(2,1)S(1)}, u32[]{:S(2)}, u32[]{:S(2)}) %all-to-all-start.2) | async-done | bytes 1310752 | tf_op jit(solution)/shard_map/all_to_all | solution.py:66
  225.2 16.6 %all-gather.5.cloned.1.call-done = bf16[1024,2048]{1,0:T(8,128)(2,1)} async-done(((bf16[128,2048]{1,0:T(8,128)(2,1)}), bf16[1024,2048]{1,0:T(8,128)(2,1)}) %all-gather.5.cloned.1.call-update) | async-done | bytes 4194320 | tf_op jit(solution)/shard_map/all_gather | solution.py:104
  241.8 7.5 %fusion.28 = f32[640,2048]{1,0:T(8,128)} fusion(bf16[1024,640]{1,0:T(8,128)(2,1)S(1)} %bitcast.41, bf16[1024,2048]{1,0:T(8,128)(2,1)} %all-gather.5.cloned.1.call-done), kind=kOutput, calls=%fused_computation.60 | convolution fusion | flops 2684354560 | bytes 10747904 | tf_op jit(solution)/shard_map/dot_general | solution.py:41
  (14 shorter events, 0.1 us)
Async XLA Ops:
  8.0 13.1 %copy-start = (bf16[320,1280]{1,0:T(8,128)(2,1)S(1)}, bf16[320,1280]{1,0:T(8,128)(2,1)}, u32[]{:S(2)}) copy-start(bf16[320,1280]{1,0:T(8,128)(2,1)} %param.15) | copy-start | bytes 2457604
  8.0 4.5 %copy-start.2 = (bf16[512,1280]{1,0:T(8,128)(2,1)S(1)}, bf16[512,1280]{1,0:T(8,128)(2,1)}, u32[]{:S(2)}) copy-start(bf16[512,1280]{1,0:T(8,128)(2,1)} %param.9) | copy-start | bytes 3932164
  8.0 6.3 %copy-start.3 = (s32[512]{0:T(512)S(1)}, s32[512]{0:T(512)}, u32[]{:S(2)}) copy-start(s32[512]{0:T(512)} %param.10) | copy-start | bytes 6148
  8.0 78.0 %all-reduce.3.cloned.1.call-start = ((), (), s32[]{:S(2)}) async-start(), calls=%async_computation.4 | async-start | bytes 2621440 | tf_op jit(solution)/shard_map/psum | solution.py:63
  21.1 2.6 copy-start.5
  23.0 112.5 %all-gather.3.cloned.1.call-start = ((), (), s32[]{:S(2)}) async-start(), calls=%async_computation.5 | async-start | bytes 23592960 | tf_op jit(solution)/shard_map/all_gather | solution.py:70
  25.0 121.4 %all-to-all-start = ((s32[8,16,1]{1,2,0:T(1,128)}), s32[8,16,1]{1,2,0:T(1,128)S(1)}, u32[]{:S(2)}, u32[]{:S(2)}) async-start(s32[8,16,1]{1,2,0:T(1,128)} %bitcast), calls=%async_computation | async-start | bytes 8192 | tf_op jit(solution)/shard_map/all_to_all | solution.py:85
  88.5 61.5 %copy-start.4 = (bf16[2048]{0:T(1024)(128)(2,1)S(1)}, bf16[2048]{0:T(1024)(128)(2,1)}, u32[]{:S(2)}) copy-start(bf16[2048]{0:T(1024)(128)(2,1)} %param.17) | copy-start | bytes 12292
  146.4 13.2 %all-to-all-start.1 = ((bf16[8,16,2048]{2,1,0:T(8,128)(2,1)}), bf16[8,16,2048]{2,1,0:T(8,128)(2,1)S(1)}, u32[]{:S(2)}, u32[]{:S(2)}) async-start(bf16[8,16,2048]{2,1,0:T(8,128)(2,1)} %bitcast.9), calls=%async_computation.1 | async-start | bytes 1048576 | tf_op jit(solution)/shard_map/all_to_all | solution.py:84
  149.9 91.9 %all-gather.5.cloned.1.call-start = ((), (), s32[]{:S(2)}) async-start(), calls=%async_computation.6 | async-start | bytes 4718592 | tf_op jit(solution)/shard_map/all_gather | solution.py:104
  199.8 25.4 %all-to-all-start.2 = ((bf16[128,8,640]{2,0,1:T(8,128)(2,1)}), bf16[128,8,640]{2,0,1:T(8,128)(2,1)S(1)}, u32[]{:S(2)}, u32[]{:S(2)}) async-start(bf16[128,8,640]{2,0,1:T(8,128)(2,1)} %copy.19), calls=%async_computation.2 | async-start | bytes 2621440 | tf_op jit(solution)/shard_map/all_to_all | solution.py:66
  241.8 7.6 %copy-start.1 = (bf16[320,1280]{1,0:T(8,128)(2,1)S(1)}, bf16[320,1280]{1,0:T(8,128)(2,1)}, u32[]{:S(2)}) copy-start(bf16[320,1280]{1,0:T(8,128)(2,1)} %param.15) | copy-start | bytes 2457604
Sparse Core Ops, SparseCore 0:
  23.2 62.7 all-reduce.2
Sparse Core Ops, SparseCore 1:
  25.4 110.0 all-gather.2
  198.2 43.5 all-gather.4
where the time goes:
time: 257 us
  waiting for transfers between devices  144 us (56%)
  matrix products  47.5 us (18%)
  blocking collectives  24.1 us (9%)
  between operations  15.7 us (6%)
  starting transfers between devices  12.4 us (5%)
  other arithmetic  9.6 us (4%)
  local copies, waits for them, and re-layouts  3.84 us (1%)
    psum x1, waiting for transfers between devices, shards(): lax.psum(partial_out.astype(jnp.bfloat16), 'tp').astype(jnp.float32)  55.8 us
    all_gather x1, waiting for transfers between devices, shards(): lax.all_gather(merger_weight, 'ctx', axis=0, tiled=True)  47 us
    all_gather x1, waiting for transfers between devices, shards(): lax.all_gather(d_merged, 'ctx', axis=0, tiled=True)  16.6 us
    all_to_all x1, waiting for transfers between devices, shards(): lax.all_to_all(merged_in, 'ctx', split_axis=1, concat_axis=0, tiled=True)  15.6 us
    dot_general x3, matrix products, contract_rows(): lax.dot_general(left, right, (((0,), (0,)), ((), ())), preferred_element_...  14.9 us
    all_to_all x1, blocking collectives, shards(): lax.all_to_all(back_rows, 'ctx', split_axis=0, concat_axis=0, tiled=True)  12.1 us
    psum x1, blocking collectives, shards(): lax.psum((jnp.sum(embedded * embedded, axis=1), jnp.sum(embedded * gained...  12 us
    dot_general x1, matrix products, shards(): jnp.dot(select_mat, merged, preferred_element_type=jnp.float32)  10.9 us
  transfers between devices with their start and end apart: 6, of which 5 were waited for; matrix products, arithmetic and copies ran while one was open for 9% of the time, Pallas kernels for 0%

commit v1 on v0

--- a/solution.py
+++ b/solution.py
@@ -60,7 +60,9 @@
     bucket_size = slots // ctx_size
     attended = window_attention(patches, window_ids, qkv_weight)
     partial_out = jnp.dot(attended, out_weight, preferred_element_type=jnp.float32)
-    summed = lax.psum(partial_out.astype(jnp.bfloat16), "tp").astype(jnp.float32)
+    summed = jnp.sum(lax.all_gather(partial_out.astype(jnp.bfloat16), "tp"), axis=0).astype(
+        jnp.float32
+    )
     hidden = (patches.astype(jnp.float32) + summed).astype(jnp.bfloat16)
     merged_in = hidden.reshape(slots, 4 * hidden.shape[1])
     columns = lax.all_to_all(merged_in, "ctx", split_axis=1, concat_axis=0, tiled=True)

time: 257 us -> 352 us (1.37)
  waiting for transfers between devices: 144 us -> 236 us
  other arithmetic: 9.6 us -> 13.6 us
    all_gather x0 -> x1, waiting for transfers between devices: none -> 93.6 us  [shards(): lax.all_gather(partial_out.astype(jnp.bfloat16), 'tp')]
    psum x1 -> x0, waiting for transfers between devices: 55.8 us -> none  [shards(): lax.psum(partial_out.astype(jnp.bfloat16), 'tp').astype(jnp.float32)]
    all_gather x1, waiting for transfers between devices: 47 us -> 101 us  [shards(): lax.all_gather(merger_weight, 'ctx', axis=0, tiled=True)]
    reduce_sum x0 -> x1, other arithmetic: none -> 4.04 us  [shards(): jnp.sum(lax.all_gather(partial_out.astype(jnp.bfloat16), 'tp'), axis=0)]
  transfers between devices with their start and end apart: 6 -> 6, of which waited for: 5 -> 5; matrix products, arithmetic and copies ran while one was open for 9% -> 8% of each run, Pallas kernels for 0% -> 0%
where the time goes in v1:
time: 352 us; the launch traced here: 351 us
  waiting for transfers between devices  236 us (67%)
  matrix products  47.3 us (13%)
  blocking collectives  23.9 us (7%)
  between operations  14 us (4%)
  other arithmetic  13.6 us (4%)
  starting transfers between devices  12.6 us (4%)
  local copies, waits for them, and re-layouts  3.84 us (1%)
    all_gather x1, waiting for transfers between devices, shards(): lax.all_gather(merger_weight, 'ctx', axis=0, tiled=True)  101 us
    all_gather x1, waiting for transfers between devices, shards(): lax.all_gather(partial_out.astype(jnp.bfloat16), 'tp')  93.6 us
    all_gather x1, waiting for transfers between devices, shards(): lax.all_gather(d_merged, 'ctx', axis=0, tiled=True)  16.5 us
    all_to_all x1, waiting for transfers between devices, shards(): lax.all_to_all(merged_in, 'ctx', split_axis=1, concat_axis=0, tiled=True)  15.8 us
    dot_general x3, matrix products, contract_rows(): lax.dot_general(left, right, (((0,), (0,)), ((), ())), preferred_element_...  14.9 us
    all_to_all x1, blocking collectives, shards(): lax.all_to_all(back_rows, 'ctx', split_axis=0, concat_axis=0, tiled=True)  12.1 us
    psum x1, blocking collectives, shards(): lax.psum((jnp.sum(embedded * embedded, axis=1), jnp.sum(embedded * gained...  11.8 us
    dot_general x1, matrix products, shards(): jnp.dot(select_mat, merged, preferred_element_type=jnp.float32)  10.8 us
  transfers between devices with their start and end apart: 6, of which 5 were waited for; matrix products, arithmetic and copies ran while one was open for 8% of the time, Pallas kernels for 0%

profile of v1, /device:TPU:0, one launch (start us, length us, event | category | flops | bytes accessed | tf_op | source)
XLA Modules:
  0.0 350.9 jit_solution(10147105845976309344)
XLA Ops:
  7.2 0.0 copy-start
  7.2 0.0 copy-start.2
  7.2 0.0 all-gather.9.cloned.1.call-start
  7.2 2.3 convolution_convert_fusion.5
  9.6 2.2 convolution_convert_fusion.4
  11.7 1.8 convolution_convert_fusion.6
  13.5 0.2 compare_and_fusion
  13.8 3.8 %fusion.27 = (f32[4,512]{1,0:T(4,128)S(1)}, f32[4,512,512]{1,2,0:T(8,128)}) fusion(pred[512,512]{0,1:T(8,128)(4,1)S(1)} %compare_and_fusion, bf16[512,4,80]{0,2,1:T(8,128)(2,1)S(1)} %bitcast.47, bf16[512,4,80]{0,2,1:T(8,128)(2,1)S(1)} %bitcast.48), kind=kOutput, calls=%fused_computation.59 | convolution fusion | flops 171966976 | bytes 5120000 | tf_op jit(solution)/shard_map/while/body/eval_jaxpr/sub | solution.py:31
  17.5 2.7 fusion.8
  20.2 0.0 copy-start.5
  20.3 1.9 convolution_convert_fusion
  22.2 0.0 all-gather.9.cloned.1.call-update
  22.2 0.0 all-gather.5.cloned.1.call-start
  22.3 0.7 all-gather.5.cloned.1.call-update
  23.0 0.1 fusion.20
  23.1 0.2 reduce_window_sum.11
  23.3 0.2 select_reduce_fusion.1
  23.4 0.1 fusion.21
  23.6 0.1 select_reduce_fusion
  23.7 0.7 select_n.47
  24.4 5.2 %all-to-all-start = ((s32[8,16,1]{1,2,0:T(1,128)}), s32[8,16,1]{1,2,0:T(1,128)S(1)}, u32[]{:S(2)}, u32[]{:S(2)}) async-start(s32[8,16,1]{1,2,0:T(1,128)} %bitcast), calls=%async_computation | async-start | bytes 8192 | tf_op jit(solution)/shard_map/all_to_all | solution.py:87
  29.6 93.6 %all-gather.9.cloned.1.call-done = bf16[2048,1280]{1,0:T(8,128)(2,1)} async-done(((bf16[512,1280]{1,0:T(8,128)(2,1)}), bf16[2048,1280]{1,0:T(8,128)(2,1)}) %all-gather.9.cloned.1.call-update) | async-done | bytes 5242896 | tf_op jit(solution)/shard_map/all_gather | solution.py:63
  123.1 4.0 %reduce_sum.61 = bf16[512,1280]{1,0:T(8,128)(2,1)S(1)} reduce(bf16[4,512,1280]{2,1,0:T(8,128)(2,1)} %bitcast.41, bf16[]{:T(256)} %constant.69.clone.1), dimensions={0}, to_apply=%region_7.8 | reduce | flops 1966080 | bytes 6553602 | tf_op jit(solution)/shard_map/reduce_sum | solution.py:63
  127.2 1.6 add_convert_fusion
  128.8 0.8 reshape.114
  129.6 0.0 copy-start.4
  129.7 101.2 %all-gather.5.cloned.1.call-done = bf16[5120,2048]{1,0:T(8,128)(2,1)} async-done(((bf16[640,2048]{1,0:T(8,128)(2,1)}), bf16[5120,2048]{1,0:T(8,128)(2,1)}) %all-gather.5.cloned.1.call-update) | async-done | bytes 20971536 | tf_op jit(solution)/shard_map/all_gather | solution.py:72
  230.8 10.8 %convolution_convert_fusion.2 = bf16[128,2048]{1,0:T(8,128)(2,1)} fusion(bf16[128,5120]{1,0:T(8,128)(2,1)S(1)} %reshape.114, bf16[5120,2048]{1,0:T(8,128)(2,1)} %all-gather.5.cloned.1.call-done, s32[128]{0:T(128)S(1)} %compare_select_fusion), kind=kOutput, calls=%fused_computation.16 | convolution fusion | flops 2752004096 | bytes 22807040 | tf_op jit(solution)/shard_map/dot_general | solution.py:81
  241.6 3.5 all-to-all-start.1
  245.1 0.2 all-gather.7.cloned.1.call-start
  245.4 0.5 broadcast.108
  245.9 0.7 reduce.4
  246.6 0.1 eq.74
  246.6 0.2 fusion.15
  246.9 7.9 %all-to-all-done.1 = bf16[8,16,2048]{2,1,0:T(8,128)(2,1)S(1)} async-done(((bf16[8,16,2048]{2,1,0:T(8,128)(2,1)}), bf16[8,16,2048]{2,1,0:T(8,128)(2,1)S(1)}, u32[]{:S(2)}, u32[]{:S(2)}) %all-to-all-start.1) | async-done | bytes 524320 | tf_op jit(solution)/shard_map/all_to_all | solution.py:86
  254.8 7.0 %multiply_reduce_fusion = (f32[1024]{0:T(1024)S(1)}, f32[1024]{0:T(1024)S(1)}, f32[1024,2048]{1,0:T(8,128)}) fusion(bf16[1024,2048]{1,0:T(8,128)(2,1)} %param.13, f32[2048]{0:T(1024)S(1)} %convert_element_type.80, bf16[1024,2048]{1,0:T(8,128)(2,1)} %param.12, bf16[128,2048]{1,0:T(8,128)(2,1)S(1)} %bitcast.44, s32[128]{0:T(128)S(1)} %eq.74, ...), kind=kOutput, calls=%fused_computation.2 | convolution fusion | flops 553777152 | bytes 17319424 | tf_op jit(solution)/shard_map/dot_general | solution.py:91
  261.8 11.8 %all-reduce = (f32[1024]{0:T(1024)S(1)}, f32[1024]{0:T(1024)S(1)}) all-reduce(f32[1024]{0:T(1024)S(1)} %get-tuple-element.15, f32[1024]{0:T(1024)S(1)} %get-tuple-element.14), channel_id=1, replica_groups=mesh['ctx'=8,'tp'=4] {'tp'}, use_global_device_ids=true, to_apply=%region_9.10 | all-reduce | flops 2048 | bytes 16384 | tf_op jit(solution)/shard_map/psum | solution.py:96
  273.6 6.2 %fusion.3 = bf16[128,2048]{1,0:T(8,128)(2,1)S(1)} fusion(f32[1024,2048]{1,0:T(8,128)} %get-tuple-element.30, bf16[1024,2048]{1,0:T(8,128)(2,1)} %param.13, f32[1024]{0:T(1024)S(1)} %get-tuple-element.17, f32[1024]{0:T(1024)S(1)} %get-tuple-element.24, f32[2048]{0:T(1024)S(1)} %convert_element_type.80, f32[1024]{0:T(1024)S(1)} %get-tuple-element.25, ...), kind=kOutput, calls=%fused_computation.14 | convolution fusion | flops 554041344 | bytes 13128192 | tf_op jit(solution)/shard_map/dot_general | solution.py:41
  279.8 12.1 %all_to_all.49 = bf16[8,16,2048]{2,1,0:T(8,128)(2,1)S(1)} all-to-all(bf16[8,16,2048]{2,1,0:T(8,128)(2,1)S(1)} %bitcast.45), channel_id=1, replica_groups=mesh['ctx'=8,'tp'=4] {'ctx'}, dimensions={0} | all-to-all | bytes 1048576 | tf_op jit(solution)/shard_map/all_to_all | solution.py:103
  291.9 1.2 convolution_convert_fusion.1
  293.1 0.0 all-gather.7.cloned.1.call-update
  293.1 0.5 all_to_all.38
  293.6 1.2 copy.20
  294.8 3.6 %all-to-all-start.2 = ((bf16[128,8,640]{2,0,1:T(8,128)(2,1)}), bf16[128,8,640]{2,0,1:T(8,128)(2,1)S(1)}, u32[]{:S(2)}, u32[]{:S(2)}) async-start(bf16[128,8,640]{2,0,1:T(8,128)(2,1)} %copy.20), calls=%async_computation.2 | async-start | bytes 2621440 | tf_op jit(solution)/shard_map/all_to_all | solution.py:68
  298.4 6.1 %multiply_convert_fusion = bf16[1024,2048]{1,0:T(8,128)(2,1)} fusion(f32[1024,2048]{1,0:T(8,128)} %get-tuple-element.30, f32[2048]{0:T(1024)S(1)} %convert_element_type.80, f32[1024]{0:T(1024)S(1)} %get-tuple-element.25), kind=kLoop, calls=%fused_computation.4 | loop fusion | flops 6291456 | bytes 12595200 | tf_op jit(solution)/shard_map/convert_element_type | solution.py:100
  304.6 15.8 %all-to-all-done.2 = bf16[128,8,640]{2,0,1:T(8,128)(2,1)S(1)} async-done(((bf16[128,8,640]{2,0,1:T(8,128)(2,1)}), bf16[128,8,640]{2,0,1:T(8,128)(2,1)S(1)}, u32[]{:S(2)}, u32[]{:S(2)}) %all-to-all-start.2) | async-done | bytes 1310752 | tf_op jit(solution)/shard_map/all_to_all | solution.py:68
  320.4 16.5 %all-gather.7.cloned.1.call-done = bf16[1024,2048]{1,0:T(8,128)(2,1)} async-done(((bf16[128,2048]{1,0:T(8,128)(2,1)}), bf16[1024,2048]{1,0:T(8,128)(2,1)}) %all-gather.7.cloned.1.call-update) | async-done | bytes 4194320 | tf_op jit(solution)/shard_map/all_gather | solution.py:106
  336.8 7.5 %fusion.28 = f32[640,2048]{1,0:T(8,128)} fusion(bf16[1024,640]{1,0:T(8,128)(2,1)S(1)} %bitcast.43, bf16[1024,2048]{1,0:T(8,128)(2,1)} %all-gather.7.cloned.1.call-done), kind=kOutput, calls=%fused_computation.60 | convolution fusion | flops 2684354560 | bytes 10747904 | tf_op jit(solution)/shard_map/dot_general | solution.py:41
  (15 shorter events, 0.1 us)
Async XLA Ops:
  7.2 13.1 %copy-start = (bf16[320,1280]{1,0:T(8,128)(2,1)S(1)}, bf16[320,1280]{1,0:T(8,128)(2,1)}, u32[]{:S(2)}) copy-start(bf16[320,1280]{1,0:T(8,128)(2,1)} %param.15) | copy-start | bytes 2457604
  7.2 4.5 %copy-start.2 = (bf16[512,1280]{1,0:T(8,128)(2,1)S(1)}, bf16[512,1280]{1,0:T(8,128)(2,1)}, u32[]{:S(2)}) copy-start(bf16[512,1280]{1,0:T(8,128)(2,1)} %param.9) | copy-start | bytes 3932164
  7.2 6.3 %copy-start.3 = (s32[512]{0:T(512)S(1)}, s32[512]{0:T(512)}, u32[]{:S(2)}) copy-start(s32[512]{0:T(512)} %param.10) | copy-start | bytes 6148
  7.2 115.9 %all-gather.9.cloned.1.call-start = ((), (), s32[]{:S(2)}) async-start(), calls=%async_computation.6 | async-start | bytes 6553600 | tf_op jit(solution)/shard_map/all_gather | solution.py:63
  20.2 2.7 copy-start.5
  22.2 208.6 %all-gather.5.cloned.1.call-start = ((), (), s32[]{:S(2)}) async-start(), calls=%async_computation.4 | async-start | bytes 23592960 | tf_op jit(solution)/shard_map/all_gather | solution.py:72
  24.4 217.3 %all-to-all-start = ((s32[8,16,1]{1,2,0:T(1,128)}), s32[8,16,1]{1,2,0:T(1,128)S(1)}, u32[]{:S(2)}, u32[]{:S(2)}) async-start(s32[8,16,1]{1,2,0:T(1,128)} %bitcast), calls=%async_computation | async-start | bytes 8192 | tf_op jit(solution)/shard_map/all_to_all | solution.py:87
  129.6 115.7 %copy-start.4 = (bf16[2048]{0:T(1024)(128)(2,1)S(1)}, bf16[2048]{0:T(1024)(128)(2,1)}, u32[]{:S(2)}) copy-start(bf16[2048]{0:T(1024)(128)(2,1)} %param.17) | copy-start | bytes 12292
  241.6 13.2 %all-to-all-start.1 = ((bf16[8,16,2048]{2,1,0:T(8,128)(2,1)}), bf16[8,16,2048]{2,1,0:T(8,128)(2,1)S(1)}, u32[]{:S(2)}, u32[]{:S(2)}) async-start(bf16[8,16,2048]{2,1,0:T(8,128)(2,1)} %bitcast.10), calls=%async_computation.1 | async-start | bytes 1048576 | tf_op jit(solution)/shard_map/all_to_all | solution.py:86
  245.1 91.7 %all-gather.7.cloned.1.call-start = ((), (), s32[]{:S(2)}) async-start(), calls=%async_computation.5 | async-start | bytes 4718592 | tf_op jit(solution)/shard_map/all_gather | solution.py:106
  294.8 25.5 %all-to-all-start.2 = ((bf16[128,8,640]{2,0,1:T(8,128)(2,1)}), bf16[128,8,640]{2,0,1:T(8,128)(2,1)S(1)}, u32[]{:S(2)}, u32[]{:S(2)}) async-start(bf16[128,8,640]{2,0,1:T(8,128)(2,1)} %copy.20), calls=%async_computation.2 | async-start | bytes 2621440 | tf_op jit(solution)/shard_map/all_to_all | solution.py:68
  336.8 7.5 %copy-start.1 = (bf16[320,1280]{1,0:T(8,128)(2,1)S(1)}, bf16[320,1280]{1,0:T(8,128)(2,1)}, u32[]{:S(2)}) copy-start(bf16[320,1280]{1,0:T(8,128)(2,1)} %param.15) | copy-start | bytes 2457604
Sparse Core Ops, SparseCore 0:
  22.3 100.7 all-gather.8
  125.0 105.7 all-gather.4
  293.3 43.5 all-gather.6
